TPU v7x, 32 devices: a whole 2x2x4 slice. The times are simulated.
32 devices in a mesh: dp: 4 (over y, core), ctx: 8 (over z, x).
Axes of the slice: x: 2, y: 2, z: 4, core: 2. Of those that a mesh axis runs over, the one named last changes fastest.
Arguments:
- tokens: bfloat16 [4, 2048, 768], P('dp', 'ctx'), may hold values from -6 to 6
- qkv_weight: bfloat16 [768, 2304], P(('dp', 'ctx')), may hold values from -0.21875 to 0.21875
- query_bias: bfloat16 [768], P(('dp', 'ctx')), may hold values from -3 to 3
- value_bias: bfloat16 [768], P(('dp', 'ctx')), may hold values from -3 to 3
- out_weight: bfloat16 [768, 768], P(('dp', 'ctx')), may hold values from -1.25 to 1.25
- out_bias: bfloat16 [768], P(('dp', 'ctx')), may hold values from -2 to 2
- attn_gain: bfloat16 [768], P(('dp', 'ctx')), may hold values from 0.5 to 1.5
- attn_shift: bfloat16 [768], P(('dp', 'ctx')), may hold values from -2 to 2
- up_weight: bfloat16 [768, 3072], P(('dp', 'ctx')), may hold values from -0.21875 to 0.21875
- up_bias: bfloat16 [3072], P(('dp', 'ctx')), may hold values from -3 to 3
- down_weight: bfloat16 [3072, 768], P(('dp', 'ctx')), may hold values from -0.109375 to 0.109375
- down_bias: bfloat16 [768], P(('dp', 'ctx')), may hold values from -2 to 2
- ffn_gain: bfloat16 [768], P(('dp', 'ctx')), may hold values from 0.5 to 1.5
- ffn_shift: bfloat16 [768], P(('dp', 'ctx')), may hold values from -2 to 2
- random_blocks: int32 [4, 32, 12, 3], P('dp', 'ctx'), may hold values from 0 to 31, as said below
- cotangent: bfloat16 [4, 2048, 768], P('dp', 'ctx'), may hold values from -6 to 6
Outputs:
- output: bfloat16 [4, 2048, 768], P('dp', 'ctx')
- tokens_grad: float32 [4, 2048, 768], P('dp', 'ctx')
- qkv_weight_grad: float32 [768, 2304], P(('dp', 'ctx'))
- query_bias_grad: float32 [768], P(('dp', 'ctx'))
- value_bias_grad: float32 [768], P(('dp', 'ctx'))
- out_weight_grad: float32 [768, 768], P(('dp', 'ctx'))
- out_bias_grad: float32 [768], P(('dp', 'ctx'))
- attn_gain_grad: float32 [768], P(('dp', 'ctx'))
- attn_shift_grad: float32 [768], P(('dp', 'ctx'))
- up_weight_grad: float32 [768, 3072], P(('dp', 'ctx'))
- up_bias_grad: float32 [3072], P(('dp', 'ctx'))
- down_weight_grad: float32 [3072, 768], P(('dp', 'ctx'))
- down_bias_grad: float32 [768], P(('dp', 'ctx'))
- ffn_gain_grad: float32 [768], P(('dp', 'ctx'))
- ffn_shift_grad: float32 [768], P(('dp', 'ctx'))
Inputs may be any that keep to these rules, and one draw needn't show every extreme that they name: `random_blocks`: key blocks j * 4 to (j + 1) * 4 - 1 of a sequence are those of index j of ctx. Over the query blocks of one sequence on one index of ctx (all heads and all 3 entries), the blocks of any one index of ctx are named at most 24 times, and exactly 24 times for one index.
All inputs are finite; a program needn't handle non-finite values.
Results may differ from a plain program's by a relative error of at most 0.014.
Values may be sent and summed in bfloat16 or wider, within the bound.
No kernel may reach another device: no remote copies, remote signals or barrier semaphores. Data moves between devices by JAX's collectives and lax.ppermute only.
A program may use at most 192 MiB of HBM per device.

v0:
```python
import jax
import jax.numpy as jnp
from jax import lax
from jax.sharding import PartitionSpec as P

H = 12
HD = 64
BLK = 64
RAND = 3


norm_eps = 1e-06
gelu_root = 0.7978845608028654
gelu_cubic = 0.044715


def extended_2(cells, sides, width):
    for axis, dim in sides:
        count = lax.axis_size(axis)
        ends = count - 1
        head = lax.slice_in_dim(cells, 0, width, axis=dim)
        tail = lax.slice_in_dim(cells, cells.shape[dim] - width, cells.shape[dim], axis=dim)
        cells = jnp.concatenate(
            [
                lax.ppermute(tail, axis, [(i, (i + 1) % count) for i in range(ends)]),
                cells,
                lax.ppermute(head, axis, [((i + 1) % count, i) for i in range(ends)]),
            ],
            axis=dim,
        )
    return cells


def joined(value, axis, join):
    pieces = jax.tree.map(lambda part: lax.all_gather(part, axis), value)
    head = jax.tree.map(lambda part: part[0], pieces)
    tail = jax.tree.map(lambda part: part[1:], pieces)
    total, _ = lax.scan(lambda total, slab: (join(total, slab), None), head, tail)
    return total


def gelu_tanh(values):
    return (
        0.5
        * values
        * (1.0 + jnp.tanh(gelu_root * (values + gelu_cubic * values * values * values)))
    )


def layer_norm(values, norm_gain, norm_shift):
    center = values - jnp.mean(values, axis=-1, keepdims=True)
    spread = jnp.mean(center * center, axis=-1, keepdims=True)
    return center * lax.rsqrt(spread + norm_eps) * norm_gain + norm_shift


def contract_rows(left_side, right_side):
    return lax.dot_general(
        left_side, right_side, (((0,), (0,)), ((), ())), preferred_element_type=jnp.float32
    )


def contract_cols(left_side, right_side):
    return lax.dot_general(
        left_side, right_side, (((1,), (1,)), ((), ())), preferred_element_type=jnp.float32
    )


def head_tiles(columns, seq_group, block_total):
    return columns.reshape(seq_group, block_total, BLK, H, HD).transpose(0, 1, 3, 2, 4)


def tile_columns(tile_block):
    lead_count = tile_block.shape[0]
    return tile_block.transpose(0, 1, 3, 2, 4).reshape(
        lead_count, tile_block.shape[1] * BLK, H * tile_block.shape[4]
    )


def merge_stats(first_side, second_side):
    largest = jnp.maximum(first_side[0], second_side[0])
    return (
        largest,
        first_side[1] * jnp.exp(first_side[0] - largest)
        + second_side[1] * jnp.exp(second_side[0] - largest),
    )


def assemble_keys(ext_seq, edge_seq, random_seq):
    blocks_dev = ext_seq.shape[0] - 2
    neighbor = jnp.stack(
        [ext_seq[0:blocks_dev], ext_seq[1 : blocks_dev + 1], ext_seq[2 : blocks_dev + 2]], axis=2
    )
    global_keys = jnp.broadcast_to(
        edge_seq.transpose(1, 0, 2, 3)[None],
        (blocks_dev, edge_seq.shape[1], 2) + edge_seq.shape[2:],
    )
    return jnp.concatenate([neighbor, global_keys, random_seq], axis=2)


def block_scores(query_seq, key_all):
    raw_scores = jnp.einsum(
        "bhqd,bhjkd->bhqjk", query_seq, key_all[..., :HD], preferred_element_type=jnp.float32
    )
    return HD ** (-0.5) * raw_scores.reshape(raw_scores.shape[:3] + (-1,))


def sparse_forward(seq_items):
    query_seq, ext_seq, edge_seq, random_seq = seq_items
    key_all = assemble_keys(ext_seq, edge_seq, random_seq)
    scores = block_scores(query_seq, key_all)
    largest = jnp.max(scores, axis=-1, keepdims=True)
    exponent = jnp.exp(scores - largest)
    row_total = jnp.sum(exponent, axis=-1, keepdims=True)
    probs_low = (
        (exponent / row_total).astype(jnp.bfloat16).reshape(scores.shape[:3] + key_all.shape[2:4])
    )
    attended = jnp.einsum(
        "bhqjk,bhjkd->bhqd", probs_low, key_all[..., HD:], preferred_element_type=jnp.float32
    )
    return (attended, (largest + jnp.log(row_total))[..., 0])


def spread_grads(grad_tiles):
    blocks_dev = grad_tiles.shape[0]
    padded = jnp.zeros(
        (blocks_dev + 2,) + grad_tiles.shape[1:2] + grad_tiles.shape[3:], jnp.float32
    )
    padded = padded.at[0:blocks_dev].add(grad_tiles[:, :, 0])
    padded = padded.at[1 : blocks_dev + 1].add(grad_tiles[:, :, 1])
    padded = padded.at[2 : blocks_dev + 2].add(grad_tiles[:, :, 2])
    edge_part = jnp.sum(grad_tiles[:, :, 3:5], axis=0).transpose(1, 0, 2, 3)
    return (padded, edge_part, grad_tiles[:, :, 5:])


def sparse_backward(seq_items):
    query_seq, ext_seq, edge_seq, random_seq, dout_seq, lse_seq = seq_items
    key_all = assemble_keys(ext_seq, edge_seq, random_seq)
    scores = block_scores(query_seq, key_all)
    attn_probs = jnp.exp(scores - lse_seq[..., None])
    tile_shape = scores.shape[:3] + key_all.shape[2:4]
    grad_probs = jnp.einsum(
        "bhqd,bhjkd->bhqjk", dout_seq, key_all[..., HD:], preferred_element_type=jnp.float32
    ).reshape(scores.shape)
    row_delta = jnp.sum(attn_probs * grad_probs, axis=-1, keepdims=True)
    grad_scores = (
        (HD ** (-0.5) * attn_probs * (grad_probs - row_delta))
        .astype(jnp.bfloat16)
        .reshape(tile_shape)
    )
    probs_low = attn_probs.astype(jnp.bfloat16).reshape(tile_shape)
    grad_query = jnp.einsum(
        "bhqjk,bhjkd->bhqd", grad_scores, key_all[..., :HD], preferred_element_type=jnp.float32
    )
    key_ext, key_edge, key_random = spread_grads(
        jnp.einsum("bhqjk,bhqd->bhjkd", grad_scores, query_seq, preferred_element_type=jnp.float32)
    )
    value_ext, value_edge, value_random = spread_grads(
        jnp.einsum("bhqjk,bhqd->bhjkd", probs_low, dout_seq, preferred_element_type=jnp.float32)
    )
    return (
        grad_query,
        jnp.concatenate([key_ext, value_ext], axis=-1),
        jnp.concatenate([key_edge, value_edge], axis=-1),
        jnp.concatenate([key_random, value_random], axis=-1),
    )


def body(
    tokens,
    qkv_weight,
    query_bias,
    value_bias,
    out_weight,
    out_bias,
    attn_gain,
    attn_shift,
    up_weight,
    up_bias,
    down_weight,
    down_bias,
    ffn_gain,
    ffn_shift,
    random_blocks,
    cotangent,
):
    (
        qkv_full,
        query_bias_full,
        value_bias_full,
        out_full,
        out_bias_full,
        attn_gain_full,
        attn_shift_full,
        up_full,
        up_bias_full,
        down_full,
        down_bias_full,
        ffn_gain_full,
        ffn_shift_full,
    ) = (
        lax.all_gather(qkv_weight, ("dp", "ctx"), axis=0, tiled=True),
        lax.all_gather(query_bias, ("dp", "ctx"), axis=0, tiled=True),
        lax.all_gather(value_bias, ("dp", "ctx"), axis=0, tiled=True),
        lax.all_gather(out_weight, ("dp", "ctx"), axis=0, tiled=True),
        lax.all_gather(out_bias, ("dp", "ctx"), axis=0, tiled=True),
        lax.all_gather(attn_gain, ("dp", "ctx"), axis=0, tiled=True),
        lax.all_gather(attn_shift, ("dp", "ctx"), axis=0, tiled=True),
        lax.all_gather(up_weight, ("dp", "ctx"), axis=0, tiled=True),
        lax.all_gather(up_bias, ("dp", "ctx"), axis=0, tiled=True),
        lax.all_gather(down_weight, ("dp", "ctx"), axis=0, tiled=True),
        lax.all_gather(down_bias, ("dp", "ctx"), axis=0, tiled=True),
        lax.all_gather(ffn_gain, ("dp", "ctx"), axis=0, tiled=True),
        lax.all_gather(ffn_shift, ("dp", "ctx"), axis=0, tiled=True),
    )
    seq_group, tok_seq, model_width = tokens.shape
    blocks_dev = tok_seq // BLK
    ctx_size = lax.axis_size("ctx")
    ctx_index = lax.axis_index("ctx")
    is_first = ctx_index == 0
    is_last = ctx_index == ctx_size - 1
    row_count = seq_group * tok_seq
    flat_tokens = tokens.reshape(row_count, model_width)
    score_scale = HD ** (-0.5)
    qkv_raw = jnp.dot(flat_tokens, qkv_full, preferred_element_type=jnp.float32)
    bias_row = jnp.concatenate(
        [query_bias_full, jnp.zeros_like(query_bias_full), value_bias_full]
    ).astype(jnp.float32)
    qkv_low = (qkv_raw + bias_row).astype(jnp.bfloat16).reshape(seq_group, tok_seq, 3 * model_width)
    query_tiles = head_tiles(qkv_low[..., :model_width], seq_group, blocks_dev)
    kv_heads = jnp.concatenate(
        [
            qkv_low[..., model_width : 2 * model_width].reshape(seq_group, tok_seq, H, HD),
            qkv_low[..., 2 * model_width :].reshape(seq_group, tok_seq, H, HD),
        ],
        axis=-1,
    ).reshape(seq_group, tok_seq, 2 * model_width)
    extended = extended_2(kv_heads, (("ctx", 1),), BLK)
    ext_pairs = extended.reshape(seq_group, blocks_dev + 2, BLK, H, 2 * HD).transpose(0, 1, 3, 2, 4)
    local_pairs = ext_pairs[:, 1 : blocks_dev + 1]
    edge_term = jnp.stack(
        [
            jnp.where(is_first, qkv_low[:, :BLK].astype(jnp.float32), 0.0),
            jnp.where(is_last, qkv_low[:, tok_seq - BLK :].astype(jnp.float32), 0.0),
        ],
        axis=1,
    )
    edge_rows = lax.psum(edge_term.astype(jnp.bfloat16), "ctx")
    edge_rows = edge_rows.reshape(seq_group, 2 * BLK, 3 * model_width)
    edge_query = head_tiles(edge_rows[..., :model_width], seq_group, 2)
    edge_pairs = jnp.concatenate(
        [
            head_tiles(edge_rows[..., model_width : 2 * model_width], seq_group, 2),
            head_tiles(edge_rows[..., 2 * model_width :], seq_group, 2),
        ],
        axis=-1,
    )
    entries = blocks_dev * H * RAND
    capacity = max(2, (4 * entries + 3 * ctx_size - 1) // (3 * ctx_size))
    owner_flat = (random_blocks // blocks_dev).reshape(seq_group, entries)
    inner_block = random_blocks % blocks_dev
    seq_ids = jnp.arange(seq_group, dtype=jnp.int32)
    head_ids = jnp.arange(H, dtype=jnp.int32)
    tile_ids = (
        (seq_ids[:, None, None, None] * blocks_dev + inner_block) * H
        + head_ids[None, None, :, None]
    ).reshape(seq_group, entries)
    owner_hot = (
        owner_flat[:, :, None] == jnp.arange(ctx_size, dtype=jnp.int32)[None, None, :]
    ).astype(jnp.int32)
    owner_rank = jnp.sum((jnp.cumsum(owner_hot, axis=1) - owner_hot) * owner_hot, axis=2)
    slot_all = (
        owner_flat * (seq_group * capacity) + seq_ids[:, None] * capacity + owner_rank
    ).reshape(-1)
    requests = (
        jnp.zeros((ctx_size * seq_group * capacity,), jnp.int32)
        .at[slot_all]
        .set(tile_ids.reshape(-1))
        .reshape(ctx_size, seq_group * capacity)
    )
    local_flat = local_pairs.reshape(seq_group * blocks_dev * H, BLK, 2 * HD)
    asked_ids = lax.all_to_all(requests, "ctx", split_axis=0, concat_axis=0, tiled=True)
    found_tiles = jnp.take(local_flat, asked_ids, axis=0)
    fetched = lax.all_to_all(found_tiles, "ctx", split_axis=0, concat_axis=0, tiled=True)
    random_pairs = jnp.take(
        fetched.reshape(ctx_size * seq_group * capacity, BLK, 2 * HD), slot_all, axis=0
    )
    random_pairs = random_pairs.reshape(seq_group, blocks_dev, H, RAND, BLK, 2 * HD)
    attended, block_lse = lax.map(
        sparse_forward, (query_tiles, ext_pairs, edge_pairs, random_pairs)
    )
    global_scores = score_scale * jnp.einsum(
        "sghqd,sbhkd->sghqbk", edge_query, local_pairs[..., :HD], preferred_element_type=jnp.float32
    )
    local_top = jnp.max(global_scores, axis=(4, 5))
    local_total = jnp.sum(jnp.exp(global_scores - local_top[..., None, None]), axis=(4, 5))
    merged_top, merged_total = joined((local_top, local_total), "ctx", merge_stats)
    global_lse = merged_top + jnp.log(merged_total)
    global_probs = jnp.exp(global_scores - global_lse[..., None, None])
    global_low = global_probs.astype(jnp.bfloat16)
    local_values = local_pairs[..., HD:]
    rounded_part = jnp.einsum(
        "sghqbk,sbhkd->sghqd", global_low, local_values, preferred_element_type=jnp.float32
    )
    exact_part = jnp.einsum(
        "sghqbk,sbhkd->sghqd",
        global_probs,
        local_values.astype(jnp.float32),
        precision=lax.Precision.HIGHEST,
    )
    global_out, global_exact = (
        lax.psum(rounded_part.astype(jnp.bfloat16), "ctx").astype(jnp.float32),
        lax.psum(exact_part.astype(jnp.bfloat16), "ctx").astype(jnp.float32),
    )
    first_rows = jnp.where(is_first, global_out[:, 0], attended[:, 0])
    attended = attended.at[:, 0].set(first_rows)
    last_rows = jnp.where(is_last, global_out[:, 1], attended[:, blocks_dev - 1])
    attended = attended.at[:, blocks_dev - 1].set(last_rows)
    attn_low = tile_columns(attended).reshape(row_count, model_width).astype(jnp.bfloat16)
    branch = jnp.dot(attn_low, out_full, preferred_element_type=jnp.float32) + out_bias_full.astype(
        jnp.float32
    )
    mid_norm, mid_pull = jax.vjp(
        layer_norm,
        flat_tokens.astype(jnp.float32) + branch,
        attn_gain_full.astype(jnp.float32),
        attn_shift_full.astype(jnp.float32),
    )
    mid_low = mid_norm.astype(jnp.bfloat16)
    pre_act = jnp.dot(mid_low, up_full, preferred_element_type=jnp.float32) + up_bias_full.astype(
        jnp.float32
    )
    activation, gelu_pull = jax.vjp(gelu_tanh, pre_act)
    act_low = activation.astype(jnp.bfloat16)
    branch_two = jnp.dot(
        act_low, down_full, preferred_element_type=jnp.float32
    ) + down_bias_full.astype(jnp.float32)
    final_norm, final_pull = jax.vjp(
        layer_norm,
        mid_norm + branch_two,
        ffn_gain_full.astype(jnp.float32),
        ffn_shift_full.astype(jnp.float32),
    )
    output = final_norm.astype(jnp.bfloat16).reshape(seq_group, tok_seq, model_width)
    grad_final, grad_ffn_gain, grad_ffn_shift = final_pull(
        cotangent.reshape(row_count, model_width).astype(jnp.float32)
    )
    down_low = grad_final.astype(jnp.bfloat16)
    grad_down_bias = jnp.sum(down_low.astype(jnp.float32), axis=0)
    grad_down = contract_rows(act_low, down_low)
    (grad_pre,) = gelu_pull(contract_cols(down_low, down_full))
    pre_low = grad_pre.astype(jnp.bfloat16)
    grad_up_bias = jnp.sum(pre_low.astype(jnp.float32), axis=0)
    grad_up = contract_rows(mid_low, pre_low)
    grad_mid = grad_final + contract_cols(pre_low, up_full)
    grad_resid, grad_attn_gain, grad_attn_shift = mid_pull(grad_mid)
    branch_low = grad_resid.astype(jnp.bfloat16)
    grad_out_bias = jnp.sum(branch_low.astype(jnp.float32), axis=0)
    grad_out = contract_rows(attn_low, branch_low)
    grad_attn = (
        contract_cols(branch_low, out_full)
        .astype(jnp.bfloat16)
        .reshape(seq_group, tok_seq, model_width)
    )
    grad_out_tiles = head_tiles(grad_attn, seq_group, blocks_dev)
    dout_term = jnp.stack(
        [
            jnp.where(is_first, grad_out_tiles[:, 0].astype(jnp.float32), 0.0),
            jnp.where(is_last, grad_out_tiles[:, blocks_dev - 1].astype(jnp.float32), 0.0),
        ],
        axis=1,
    )
    global_dout = lax.psum(dout_term.astype(jnp.bfloat16), "ctx")
    block_ids = jnp.arange(blocks_dev, dtype=jnp.int32)
    dropped = (block_ids == 0) & is_first | (block_ids == blocks_dev - 1) & is_last
    dout_kept = jnp.where(
        dropped[None, :, None, None, None], jnp.zeros_like(grad_out_tiles), grad_out_tiles
    )
    grad_query, ext_grads, edge_key_grads, random_grads = lax.map(
        sparse_backward, (query_tiles, ext_pairs, edge_pairs, random_pairs, dout_kept, block_lse)
    )
    global_dprobs = jnp.einsum(
        "sghqd,sbhkd->sghqbk", global_dout, local_values, preferred_element_type=jnp.float32
    )
    global_delta = jnp.sum(global_dout.astype(jnp.float32) * global_exact, axis=-1)
    global_dscores = (
        score_scale * global_probs * (global_dprobs - global_delta[..., None, None])
    ).astype(jnp.bfloat16)
    global_dquery = jnp.einsum(
        "sghqbk,sbhkd->sghqd",
        global_dscores,
        local_pairs[..., :HD],
        preferred_element_type=jnp.float32,
    )
    global_dkeys = jnp.einsum(
        "sghqbk,sghqd->sbhkd", global_dscores, edge_query, preferred_element_type=jnp.float32
    )
    global_dvalues = jnp.einsum(
        "sghqbk,sghqd->sbhkd", global_low, global_dout, preferred_element_type=jnp.float32
    )
    rim_grads = jnp.stack([ext_grads[:, 0], ext_grads[:, blocks_dev + 1]], axis=1)
    rim_halo = extended_2(rim_grads.astype(jnp.bfloat16), (("ctx", 1),), 1).astype(rim_grads.dtype)
    local_grads = ext_grads[:, 1 : blocks_dev + 1] + jnp.concatenate(
        [global_dkeys, global_dvalues], axis=-1
    )
    local_grads = local_grads.at[:, 0].add(rim_halo[:, 0])
    local_grads = local_grads.at[:, blocks_dev - 1].add(rim_halo[:, 3])
    outgoing = (
        jnp.zeros((ctx_size * seq_group * capacity, BLK, 2 * HD), jnp.float32)
        .at[slot_all]
        .set(random_grads.reshape(seq_group * entries, BLK, 2 * HD))
        .reshape(ctx_size, seq_group * capacity, BLK, 2 * HD)
    )
    returned = lax.all_to_all(
        outgoing.astype(jnp.bfloat16), "ctx", split_axis=0, concat_axis=0, tiled=True
    ).astype(outgoing.dtype)
    local_grads = (
        local_grads.reshape(seq_group * blocks_dev * H, BLK * 2 * HD)
        .at[asked_ids.reshape(-1)]
        .add(returned.reshape(-1, BLK * 2 * HD))
        .reshape(seq_group, blocks_dev, H, BLK, 2 * HD)
    )
    edge_grad_term = jnp.concatenate(
        [
            tile_columns(global_dquery),
            tile_columns(edge_key_grads[..., :HD]),
            tile_columns(edge_key_grads[..., HD:]),
        ],
        axis=-1,
    )
    edge_sums = lax.psum(edge_grad_term.astype(jnp.bfloat16), "ctx").astype(jnp.float32)
    grad_qkv_rows = jnp.concatenate(
        [
            tile_columns(grad_query),
            tile_columns(local_grads[..., :HD]),
            tile_columns(local_grads[..., HD:]),
        ],
        axis=-1,
    )
    grad_qkv_rows = grad_qkv_rows.at[:, :BLK].add(jnp.where(is_first, edge_sums[:, :BLK], 0.0))
    grad_qkv_rows = grad_qkv_rows.at[:, tok_seq - BLK :].add(
        jnp.where(is_last, edge_sums[:, BLK:], 0.0)
    )
    qkv_grad_low = grad_qkv_rows.reshape(row_count, 3 * model_width).astype(jnp.bfloat16)
    column_sums = jnp.sum(qkv_grad_low.astype(jnp.float32), axis=0)
    grad_query_bias = column_sums[:model_width]
    grad_value_bias = column_sums[2 * model_width :]
    grad_qkv = contract_rows(flat_tokens, qkv_grad_low)
    tokens_grad = (grad_resid + contract_cols(qkv_grad_low, qkv_full)).reshape(
        seq_group, tok_seq, model_width
    )
    every_shard = (
        lax.psum_scatter(grad_qkv, ("dp", "ctx"), scatter_dimension=0, tiled=True),
        lax.psum_scatter(grad_query_bias, ("dp", "ctx"), scatter_dimension=0, tiled=True),
        lax.psum_scatter(grad_value_bias, ("dp", "ctx"), scatter_dimension=0, tiled=True),
        lax.psum_scatter(grad_out, ("dp", "ctx"), scatter_dimension=0, tiled=True),
        lax.psum_scatter(grad_out_bias, ("dp", "ctx"), scatter_dimension=0, tiled=True),
        lax.psum_scatter(grad_attn_gain, ("dp", "ctx"), scatter_dimension=0, tiled=True),
        lax.psum_scatter(grad_attn_shift, ("dp", "ctx"), scatter_dimension=0, tiled=True),
        lax.psum_scatter(grad_up, ("dp", "ctx"), scatter_dimension=0, tiled=True),
        lax.psum_scatter(grad_up_bias, ("dp", "ctx"), scatter_dimension=0, tiled=True),
        lax.psum_scatter(grad_down, ("dp", "ctx"), scatter_dimension=0, tiled=True),
        lax.psum_scatter(grad_down_bias, ("dp", "ctx"), scatter_dimension=0, tiled=True),
        lax.psum_scatter(grad_ffn_gain, ("dp", "ctx"), scatter_dimension=0, tiled=True),
        lax.psum_scatter(grad_ffn_shift, ("dp", "ctx"), scatter_dimension=0, tiled=True),
    )
    attn_shards = every_shard[:7]
    ffn_shards = every_shard[7:]
    return (output, tokens_grad) + tuple(attn_shards) + tuple(ffn_shards)


def solution(mesh):
    return jax.shard_map(
        body,
        mesh=mesh,
        in_specs=(
            P("dp", "ctx", None),
            P(("dp", "ctx"), None),
            P(("dp", "ctx")),
            P(("dp", "ctx")),
            P(("dp", "ctx"), None),
            P(("dp", "ctx")),
            P(("dp", "ctx")),
            P(("dp", "ctx")),
            P(("dp", "ctx"), None),
            P(("dp", "ctx")),
            P(("dp", "ctx"), None),
            P(("dp", "ctx")),
            P(("dp", "ctx")),
            P(("dp", "ctx")),
            P("dp", "ctx", None, None),
            P("dp", "ctx", None),
        ),
        out_specs=(
            P("dp", "ctx", None),
            P("dp", "ctx", None),
            P(("dp", "ctx"), None),
            P(("dp", "ctx")),
            P(("dp", "ctx")),
            P(("dp", "ctx"), None),
            P(("dp", "ctx")),
            P(("dp", "ctx")),
            P(("dp", "ctx")),
            P(("dp", "ctx"), None),
            P(("dp", "ctx")),
            P(("dp", "ctx"), None),
            P(("dp", "ctx")),
            P(("dp", "ctx")),
            P(("dp", "ctx")),
        ),
        check_vma=False,
    )
```

profile of v0, /device:TPU:0, one launch (start us, length us, event | category | flops | bytes accessed | tf_op | source)
XLA Modules:
  0.0 1279.6 jit_solution(11488793250883467905)
XLA Ops:
  15.5 42.6 %all-reduce.22 = (bf16[768]{0:T(1024)(128)(2,1)S(1)}, bf16[768]{0:T(1024)(128)(2,1)S(1)}, bf16[768]{0:T(1024)(128)(2,1)}, bf16[768]{0:T(1024)(128)(2,1)}, bf16[7...) all-reduce(bf16[768]{0:T(1024)(128)(2,1)S(1)} %dynamic-update-slice, ...), channel_id=1, replica_groups=mesh['dp'=4,'ctx'=8] {'dp','ctx'}, use_global_device_ids=true, to_apply=%add.4 | all-reduce | flops 9216 | bytes 36864
  58.2 15.8 %all-gather.7.cloned.1.call-done = bf16[768,2304]{1,0:T(8,128)(2,1)} async-done(((bf16[24,2304]{1,0:T(8,128)(2,1)}), bf16[768,2304]{1,0:T(8,128)(2,1)}) %all-gather.7.cloned.1.call-update) | async-done | bytes 3538960 | tf_op jit(solution)/shard_map/all_gather | solution.py:201
  92.1 10.3 collective-permute-done
  111.4 49.9 %all-reduce.29.cloned.1.call-done = bf16[1,128,2304]{1,2,0:T(8,128)(2,1)} async-done(((bf16[1,128,2304]{1,2,0:T(8,128)(2,1)}), bf16[1,128,2304]{1,2,0:T(8,128)(2,1)}) %all-reduce.29.cloned.1.call-update) | async-done | bytes 589840 | tf_op jit(solution)/shard_map/psum | solution.py:247
  166.0 30.5 %all-gather = f32[16,12,64]{2,1,0:T(8,128)S(1)} all-gather(f32[2,12,64]{2,1,0:T(8,128)S(1)} %copy.191), channel_id=2, replica_groups=mesh['dp'=4,'ctx'=8] {'ctx'}, dimensions={0}, use_global_device_ids=true | all-gather | bytes 55296 | tf_op jit(solution)/shard_map/all_gather | solution.py:35
  197.2 30.5 %all-gather.1 = f32[16,12,64]{2,1,0:T(8,128)S(1)} all-gather(f32[2,12,64]{2,1,0:T(8,128)S(1)} %copy.192), channel_id=3, replica_groups=mesh['dp'=4,'ctx'=8] {'ctx'}, dimensions={0}, use_global_device_ids=true | all-gather | bytes 55296 | tf_op jit(solution)/shard_map/all_gather | solution.py:35
  239.1 10.1 all_to_all.25
  284.4 34.9 %all-to-all-done.1 = bf16[8,24,64,128]{3,2,1,0:T(8,128)(2,1)} async-done(((bf16[8,24,64,128]{3,2,1,0:T(8,128)(2,1)}), bf16[8,24,64,128]{3,2,1,0:T(8,128)(2,1)}, u32[]{:S(2)}, u32[]{:S(2)}) %all-to-all-start.1) | async-done | bytes 3145760 | tf_op jit(solution)/shard_map/all_to_all | solution.py:283
  336.3 10.9 fusion.56
  350.7 33.4 %all-gather.9.cloned.1.call-done = bf16[768,768]{1,0:T(8,128)(2,1)} async-done(((bf16[24,768]{1,0:T(8,128)(2,1)}), bf16[768,768]{1,0:T(8,128)(2,1)}) %all-gather.9.cloned.1.call-update) | async-done | bytes 1179664 | tf_op jit(solution)/shard_map/all_gather | solution.py:204
  386.2 63.3 %all-gather.11.cloned.1.call-done = bf16[768,3072]{1,0:T(8,128)(2,1)} async-done(((bf16[24,3072]{1,0:T(8,128)(2,1)}), bf16[768,3072]{1,0:T(8,128)(2,1)}) %all-gather.11.cloned.1.call-update) | async-done | bytes 4718608 | tf_op jit(solution)/shard_map/all_gather | solution.py:208
  455.0 59.9 %all-gather.13.cloned.1.call-done = bf16[3072,768]{1,0:T(8,128)(2,1)} async-done(((bf16[96,768]{1,0:T(8,128)(2,1)}), bf16[3072,768]{1,0:T(8,128)(2,1)}) %all-gather.13.cloned.1.call-update) | async-done | bytes 4718608 | tf_op jit(solution)/shard_map/all_gather | solution.py:210
  534.9 11.7 multiply_reduce_fusion
  546.6 11.2 fusion.4
  557.9 10.7 multiply_convert_fusion
  585.7 65.4 %all-reduce.35.cloned.1.call-done = (bf16[1,2,12,64,64]{4,3,2,1,0:T(8,128)(2,1)}, bf16[1,2,12,64,64]{4,3,2,1,0:T(8,128)(2,1)}) async-done(((bf16[1,2,12,64,64]{4,3,2,1,0:T(8,128)(2,1)}, bf16[1,2,12,64,64]{4,3,2,1,0:T(8,128)(2,1)}), (bf16[1,2,12,64,64]{4,3,2,1,0:T(8,128)(2,1)}, bf16[1,2,12,64,64]{4,3,2,1,0:T(8,128)(2,1)})) %all-reduce.35.cloned.1.call-update) | async-done | bytes 393232 | tf_op jit(solution)/shard_map/psum | solution.py:372
  684.1 21.8 %scatter_fusion = f32[192,64,128]{2,1,0:T(8,128)} fusion(f32[192,64,128]{2,1,0:T(8,128)} %broadcast_in_dim.154, s32[144]{0:T(256)S(1)} %bitcast.421, f32[144,64,128]{2,1,0:T(8,128)} %bitcast.390), kind=kCustom, calls=%fused_computation.3 | custom fusion | bytes 14156352 | tf_op jit(solution)/shard_map/scatter | solution.py:410
  755.8 37.2 %all-to-all-done.2 = bf16[8,24,64,128]{3,2,1,0:T(8,128)(2,1)S(1)} async-done(((bf16[8,24,64,128]{3,2,1,0:T(8,128)(2,1)}), bf16[8,24,64,128]{3,2,1,0:T(8,128)(2,1)S(1)}, u32[]{:S(2)}, u32[]{:S(2)}) %all-to-all-start.2) | async-done | bytes 3145760 | tf_op jit(solution)/shard_map/all_to_all | solution.py:413
  796.4 16.8 %scatter_custom_fusion.2 = f32[48,8192]{1,0:T(8,128)} fusion(f32[48,8192]{1,0:T(8,128)} %bitcast.403, s32[192]{0:T(256)S(1)} %bitcast.424, f32[24,8,64,128]{3,2,1,0:T(8,128)} %convert.64), kind=kCustom, calls=%fused_computation.19 | custom fusion | flops 1572864 | bytes 7864320 | tf_op jit(solution)/shard_map/scatter-add | solution.py:419
  835.9 8.1 copy.286
  845.8 46.5 %all-reduce.21 = (f32[768]{0:T(1024)S(1)}, f32[768]{0:T(1024)S(1)}, f32[768]{0:T(1024)S(1)}, f32[768]{0:T(1024)S(1)}, f32[768]{0:T(1024)S(1)}, /*index=5*/f32[30...) all-reduce(f32[768]{0:T(1024)S(1)} %get-tuple-element.416, ...), channel_id=5, replica_groups=mesh['dp'=4,'ctx'=8] {'dp','ctx'}, use_global_device_ids=true, to_apply=%region_31.32.clone | all-reduce | flops 9216 | bytes 73728
  901.8 103.9 %reduce-scatter.9.cloned.1.call-done = f32[24,3072]{1,0:T(8,128)} async-done(((f32[768,3072]{1,0:T(8,128)}), f32[24,3072]{1,0:T(8,128)}) %reduce-scatter.9.cloned.1.call-update) | async-done | bytes 294928 | tf_op jit(solution)/shard_map/reduce_scatter | solution.py:459
  1005.7 141.3 %reduce-scatter.11.cloned.1.call-done = f32[96,768]{1,0:T(8,128)} async-done(((f32[3072,768]{1,0:T(8,128)}), f32[96,768]{1,0:T(8,128)}) %reduce-scatter.11.cloned.1.call-update) | async-done | bytes 294928 | tf_op jit(solution)/shard_map/reduce_scatter | solution.py:461
  1147.0 125.2 %reduce-scatter.13.cloned.1.call-done = f32[24,2304]{1,0:T(8,128)} async-done(((f32[768,2304]{1,0:T(8,128)}), f32[24,2304]{1,0:T(8,128)}) %reduce-scatter.13.cloned.1.call-update) | async-done | bytes 221200
  (394 shorter events, 271.8 us)
Async XLA Ops:
  7.2 66.8 %all-gather.7.cloned.1.call-start = ((), (), s32[]{:S(2)}) async-start(), calls=%async_computation.7 | async-start | bytes 3649536 | tf_op jit(solution)/shard_map/all_gather | solution.py:201
  7.9 153.3 %all-reduce.29.cloned.1.call-start = ((), (), s32[]{:S(2)}) async-start(), calls=%async_computation.8 | async-start | bytes 1179648 | tf_op jit(solution)/shard_map/psum | solution.py:247
  78.7 13.5 %collective-permute-start.1 = (bf16[1,64,1536]{1,2,0:T(8,128)(2,1)}, bf16[1,64,1536]{1,2,0:T(8,128)(2,1)}, u32[]{:S(2)}, u32[]{:S(2)}) collective-permute-start(bf16[1,64,1536]{1,2,0:T(8,128)(2,1)} %get-tuple-element.409), channel_id=1, source_target_pairs={{1,0},{2,1},{3,2},{4,3},{5,4},{6,5},{7,6},{9,8},{10,9},{11,10},{12... | collective-permute-start | bytes 589832 | tf_op jit(solution)/shard_map/ppermute | solution.py:27
  79.9 22.5 %collective-permute-start = (bf16[1,64,1536]{1,2,0:T(8,128)(2,1)S(1)}, bf16[1,64,1536]{1,2,0:T(8,128)(2,1)}, u32[]{:S(2)}, u32[]{:S(2)}) collective-permute-start(bf16[1,64,1536]{1,2,0:T(8,128)(2,1)S(1)} %get-tuple-element.408), channel_id=1, source_target_pairs={{0,1},{1,2},{2,3},{3,4},{4,5},{5,6},{6,7},{8,9},{9,10},{10,11},{11... | collective-permute-start | bytes 589832 | tf_op jit(solution)/shard_map/ppermute | solution.py:25
  86.5 260.8 %all-reduce.31.cloned.1.call-start = ((), (), s32[]{:S(2)}) async-start(), calls=%async_computation.9 | async-start | bytes 786432 | tf_op jit(solution)/shard_map/psum | solution.py:311
  111.4 121.1 %copy-start.29 = (bf16[4,12,64,64,1]{3,2,1,0,4:T(8,128)(2,1)}, bf16[4,12,64,64,1]{3,2,1,0,4:T(8,128)(2,1)S(1)}, u32[]{:S(2)}) copy-start(bf16[4,12,64,64,1]{3,2,1,0,4:T(8,128)(2,1)S(1)} %get-tuple-element.398) | copy-start | bytes 1179652
  235.0 149.0 %all-gather.9.cloned.1.call-start = ((), (), s32[]{:S(2)}) async-start(), calls=%async_computation.10 | async-start | bytes 1216512 | tf_op jit(solution)/shard_map/all_gather | solution.py:204
  235.6 213.9 %all-gather.11.cloned.1.call-start = ((), (), s32[]{:S(2)}) async-start(), calls=%async_computation.11 | async-start | bytes 4866048 | tf_op jit(solution)/shard_map/all_gather | solution.py:208
  255.3 64.0 %all-to-all-start.1 = ((bf16[8,24,64,128]{3,2,1,0:T(8,128)(2,1)}), bf16[8,24,64,128]{3,2,1,0:T(8,128)(2,1)}, u32[]{:S(2)}, u32[]{:S(2)}) async-start(bf16[8,24,64,128]{3,2,1,0:T(8,128)(2,1)} %broadcast_select_fusion), calls=%async_computation.1 | async-start | bytes 6291456 | tf_op jit(solution)/shard_map/all_to_all | solution.py:283
  259.8 255.1 %all-gather.13.cloned.1.call-start = ((), (), s32[]{:S(2)}) async-start(), calls=%async_computation.12 | async-start | bytes 4866048 | tf_op jit(solution)/shard_map/all_gather | solution.py:210
  260.4 390.6 %all-reduce.35.cloned.1.call-start = ((), (), s32[]{:S(2)}) async-start(), calls=%async_computation.18 | async-start | bytes 1572864 | tf_op jit(solution)/shard_map/psum | solution.py:372
  350.7 104.3 %copy-start.22 = (bf16[256,768]{0,1:T(8,128)(2,1)}, bf16[256,768]{0,1:T(8,128)(2,1)S(1)}, u32[]{:S(2)}) copy-start(bf16[256,768]{0,1:T(8,128)(2,1)S(1)} %convert_element_type.241) | copy-start | bytes 1179652
  385.9 144.2 %copy-start.5 = (f32[256,768]{1,0:T(8,128)}, f32[256,768]{1,0:T(8,128)S(1)}, u32[]{:S(2)}) copy-start(f32[256,768]{1,0:T(8,128)S(1)} %get-tuple-element.423) | copy-start | bytes 2359300
  385.9 144.1 %copy-start.40 = (f32[256]{0:T(256)}, f32[256]{0:T(256)S(1)}, u32[]{:S(2)}) copy-start(f32[256]{0:T(256)S(1)} %broadcast_multiply_fusion.2) | copy-start | bytes 3076
  386.2 143.9 %copy-start.47 = (f32[256]{0:T(256)}, f32[256]{0:T(256)S(1)}, u32[]{:S(2)}) copy-start(f32[256]{0:T(256)S(1)} %fusion.144) | copy-start | bytes 3076
  386.2 128.7 %copy-start.55 = (f32[768]{0:T(1024)S(1)}, f32[768]{0:T(1024)}, u32[]{:S(2)}) copy-start(f32[768]{0:T(1024)} %convert_element_type.248) | copy-start | bytes 9220
  577.2 176.4 %all-reduce.33.cloned.1.call-start = ((), (), s32[]{:S(2)}) async-start(), calls=%async_computation.13 | async-start | bytes 1179648 | tf_op jit(solution)/shard_map/psum | solution.py:430
  658.0 243.8 %reduce-scatter.7.cloned.1.call-start = ((), (), s32[]{:S(2)}) async-start(), calls=%async_computation.14 | async-start | bytes 2433024 | tf_op jit(solution)/shard_map/reduce_scatter | solution.py:455
  660.4 345.3 %reduce-scatter.9.cloned.1.call-start = ((), (), s32[]{:S(2)}) async-start(), calls=%async_computation.15 | async-start | bytes 9732096 | tf_op jit(solution)/shard_map/reduce_scatter | solution.py:459
  665.7 481.4 %reduce-scatter.11.cloned.1.call-start = ((), (), s32[]{:S(2)}) async-start(), calls=%async_computation.16 | async-start | bytes 9732096 | tf_op jit(solution)/shard_map/reduce_scatter | solution.py:461
  711.1 81.9 %all-to-all-start.2 = ((bf16[8,24,64,128]{3,2,1,0:T(8,128)(2,1)}), bf16[8,24,64,128]{3,2,1,0:T(8,128)(2,1)S(1)}, u32[]{:S(2)}, u32[]{:S(2)}) async-start(bf16[8,24,64,128]{3,2,1,0:T(8,128)(2,1)} %bitcast.393), calls=%async_computation.2 | async-start | bytes 6291456 | tf_op jit(solution)/shard_map/all_to_all | solution.py:413
  714.7 557.6 %reduce-scatter.13.cloned.1.call-start = ((), (), s32[]{:S(2)}) async-start(), calls=%async_computation.17 | async-start | bytes 7299072
  739.5 8.9 collective-permute-start.3
  741.1 10.3 collective-permute-start.2
  (66 other events, 889.0 us)
Sparse Core Ops, SparseCore 0:
  11.0 62.9 all-gather.6
  86.6 74.5 all-reduce.28
  235.2 92.7 all-reduce.30
  330.8 53.1 all-gather.8
  386.9 62.6 all-gather.10
  452.4 62.4 all-gather.12
  577.3 73.6 all-reduce.34
  658.1 86.0 all-reduce.32
  750.1 113.8 reduce-scatter.6
  871.3 134.3 reduce-scatter.8
  1012.2 134.7 reduce-scatter.10
  1154.1 118.1 reduce-scatter.12
where the time goes:
time: 1290 us; the launch traced here: 1280 us
  waiting for transfers between devices  752 us (58%)
  blocking collectives  160 us (12%)
  local copies, waits for them, and re-layouts  135 us (10%)
  matrix products  105 us (8%)
  other arithmetic  89.5 us (7%)
  starting transfers between devices  22.1 us (2%)
  between operations  16 us (1%)
    reduce_scatter x1, waiting for transfers between devices, body(): lax.psum_scatter(grad_down, ('dp', 'ctx'), scatter_dimension=0, tiled=True)  141 us
    unnamed x13, waiting for transfers between devices  128 us
    reduce_scatter x1, waiting for transfers between devices, body(): lax.psum_scatter(grad_up, ('dp', 'ctx'), scatter_dimension=0, tiled=True)  104 us
    unnamed x2, blocking collectives  89.1 us
    psum x1, waiting for transfers between devices, body(): global_dout = lax.psum(dout_term.astype(jnp.bfloat16), 'ctx')  65.4 us
    all_gather x1, waiting for transfers between devices, body(): lax.all_gather(up_weight, ('dp', 'ctx'), axis=0, tiled=True)  63.3 us
    all_gather x2, blocking collectives, joined(): pieces = jax.tree.map(lambda part: lax.all_gather(part, axis), value)  61 us
    all_gather x1, waiting for transfers between devices, body(): lax.all_gather(down_weight, ('dp', 'ctx'), axis=0, tiled=True)  59.9 us
  transfers between devices with their start and end apart: 18, of which 14 were waited for; matrix products, arithmetic and copies ran while one was open for 18% of the time, Pallas kernels for 0%

commit v1 on v0

v1 whole, which is shorter than its diff:
```python
import functools

import jax
import jax.numpy as jnp
from jax import lax
from jax.experimental import pallas as pl
from jax.experimental.pallas import tpu as pltpu
from jax.sharding import Mesh, PartitionSpec as P

H = 12
HD = 64
BLK = 64
RAND = 3
GROUPS = 4
PER_GROUP = 3
PAD_ROWS = 16
EXTRA = 128
VMEM_BYTES = 56 * 1024 * 1024

bf16 = jnp.bfloat16
f32 = jnp.float32

norm_eps = 1e-06
gelu_root = 0.7978845608028654
gelu_cubic = 0.044715

ALL = ("y", "core", "z", "x")
CTX = ("z", "x")


def gelu_tanh(values):
    return (
        0.5
        * values
        * (1.0 + jnp.tanh(gelu_root * (values + gelu_cubic * values * values * values)))
    )


def layer_norm(values, norm_gain, norm_shift):
    center = values - jnp.mean(values, axis=-1, keepdims=True)
    spread = jnp.mean(center * center, axis=-1, keepdims=True)
    return center * lax.rsqrt(spread + norm_eps) * norm_gain + norm_shift


def contract_rows(left_side, right_side):
    return lax.dot_general(
        left_side, right_side, (((0,), (0,)), ((), ())), preferred_element_type=f32
    )


def contract_cols(left_side, right_side):
    return lax.dot_general(
        left_side, right_side, (((1,), (1,)), ((), ())), preferred_element_type=f32
    )


def plain(left_side, right_side):
    return jnp.dot(left_side, right_side, preferred_element_type=f32)


def heads_of(index, ranks):
    group, rank = index // ranks, index % ranks
    first = PER_GROUP * group + (0 if rank < ranks // 2 else 1)
    return first, PER_GROUP * group + 2


def qkv_kernel(count, ranks, x_ref, w_ref, b_ref, rnd_ref, out_ref):
    tok, width = x_ref.shape
    x = x_ref[...]
    for part in range(3):
        rows = plain(x, w_ref[:, part * width : (part + 1) * width]) + b_ref[part : part + 1, :]
        rows = rows.astype(bf16)
        for j in range(count):
            first, shared = heads_of(j, ranks)
            out_ref[j, 0:tok, part * 128 : (part + 1) * 128] = jnp.concatenate(
                [rows[:, first * HD : (first + 1) * HD], rows[:, shared * HD : (shared + 1) * HD]],
                axis=1,
            )
    for j in range(count):
        out_ref[j, tok : tok + PAD_ROWS, :] = rnd_ref[j]


def qkv_chunks(count, ranks, tokens, weights, bias, rnd):
    tok = tokens.shape[0]
    return pl.pallas_call(
        functools.partial(qkv_kernel, count, ranks),
        out_shape=jax.ShapeDtypeStruct((count, tok + PAD_ROWS, 384), bf16),
        in_specs=[pl.BlockSpec(memory_space=pltpu.VMEM)] * 4,
        out_specs=pl.BlockSpec(memory_space=pltpu.VMEM),
        compiler_params=pltpu.CompilerParams(vmem_limit_bytes=VMEM_BYTES),
        name="qkv_chunks",
    )(tokens, weights, bias, rnd)


class Plan:
    def __init__(self, count, ranks, blocks):
        self.count, self.ranks, self.blocks = count, ranks, blocks
        self.steps = (ranks // 2, ranks)
        self.owners = (count // self.steps[0], count // self.steps[1])
        self.total = count * blocks
        self.units = (self.owners[0] + self.owners[1]) * blocks
        self.stride = blocks * BLK + PAD_ROWS

    def key_rows(self, block):
        return pl.multiple_of(
            (block // self.blocks) * self.stride + (block % self.blocks) * BLK, 16
        )

    def sum_rows(self, block):
        return pl.multiple_of(block * BLK, BLK)

    def unit(self, half, turn, inner):
        return (half * self.owners[0] + turn) * self.blocks + inner

    def named(self, half, owner, inner, rand_ref):
        block = owner * self.blocks + inner
        ids = [
            jnp.maximum(block - 1, 0),
            block,
            jnp.minimum(block + 1, self.total - 1),
            0,
            self.total - 1,
        ]
        for t in range(RAND):
            ids.append(rand_ref[(block * 2 + half) * RAND + t])
        return ids


def lane_half(rows, half):
    lane = lax.broadcasted_iota(jnp.int32, (rows, 128), 1)
    return (lane < HD) if half == 0 else (lane >= HD)


def only_half(values, half):
    return jnp.where(lane_half(values.shape[0], half), values, jnp.zeros_like(values))


def attn_forward_kernel(plan, rand_ref, rank_ref, kv_ref, out_ref, lse_ref, score_ref):
    tok = plan.blocks * BLK
    rank = rank_ref[0]
    out_ref[...] = jnp.zeros_like(out_ref)

    def emit(half, owner, inner, unit, attended, lse):
        lanes = pl.ds(half * HD, HD)
        out_ref[pl.ds(pl.multiple_of(owner * tok + inner * BLK, BLK), BLK), lanes] = attended[
            :, half * HD : (half + 1) * HD
        ].astype(bf16)
        lse_ref[pl.ds(pl.multiple_of(unit * BLK, BLK), BLK), :] = jnp.broadcast_to(lse, (BLK, 128))

    def query(half, owner, inner):
        rows = pl.multiple_of(owner * plan.stride + inner * BLK, 16)
        return only_half(kv_ref[pl.ds(rows, BLK), 0:128], half) * 0.125

    for half in range(2):
        step = plan.steps[half]
        offset = lax.rem(rank, step) if step > 1 else 0

        def turn_body(turn, carry, half=half, step=step, offset=offset):
            owner = turn * step + offset
            for inner in range(plan.blocks):
                ids = plan.named(half, owner, inner, rand_ref)
                rows = [plan.key_rows(i) for i in ids]
                keys = jnp.concatenate([kv_ref[pl.ds(r, BLK), 128:256] for r in rows], axis=0)
                values = jnp.concatenate([kv_ref[pl.ds(r, BLK), 256:384] for r in rows], axis=0)
                scores = contract_cols(query(half, owner, inner), keys)
                top = jnp.max(scores, axis=-1, keepdims=True)
                grown = jnp.exp(scores - top)
                total = jnp.sum(grown, axis=-1, keepdims=True)
                probs = (grown * (1.0 / total)).astype(bf16)
                attended = plain(probs, values)
                emit(half, owner, inner, plan.unit(half, turn, inner), attended, top + jnp.log(total))
            return carry

        lax.fori_loop(0, plan.owners[half], turn_body, 0)

    for half in range(2):
        step = plan.steps[half]
        for owner, inner in ((0, 0), (plan.count - 1, plan.blocks - 1)):

            def whole(half=half, step=step, owner=owner, inner=inner):
                q = query(half, owner, inner)

                def score_body(o, top):
                    rows = pl.multiple_of(o * plan.stride, 16)
                    part = contract_cols(q, kv_ref[pl.ds(rows, tok), 128:256])
                    score_ref[o] = part
                    return jnp.maximum(top, jnp.max(part, axis=-1, keepdims=True))

                top = lax.fori_loop(
                    0, plan.count, score_body, jnp.full((BLK, 1), -jnp.inf, f32)
                )

                def sum_body(o, total):
                    grown = jnp.exp(score_ref[o] - top)
                    score_ref[o] = grown
                    return total + jnp.sum(grown, axis=-1, keepdims=True)

                total = lax.fori_loop(0, plan.count, sum_body, jnp.zeros((BLK, 1), f32))
                scale = 1.0 / total

                def value_body(o, attended):
                    rows = pl.multiple_of(o * plan.stride, 16)
                    probs = (score_ref[o] * scale).astype(bf16)
                    return attended + plain(probs, kv_ref[pl.ds(rows, tok), 256:384])

                attended = lax.fori_loop(0, plan.count, value_body, jnp.zeros((BLK, 128), f32))
                unit = plan.unit(half, owner // step, inner)
                emit(half, owner, inner, unit, attended, top + jnp.log(total))

            if step == 1:
                whole()
            else:
                pl.when(lax.rem(rank, step) == owner % step)(whole)


def attn_forward(plan, rand, rank, kv):
    tok = plan.blocks * BLK
    return pl.pallas_call(
        functools.partial(attn_forward_kernel, plan),
        out_shape=(
            jax.ShapeDtypeStruct((plan.count * tok, 128), bf16),
            jax.ShapeDtypeStruct((plan.units * BLK, 128), f32),
        ),
        in_specs=[
            pl.BlockSpec(memory_space=pltpu.SMEM),
            pl.BlockSpec(memory_space=pltpu.SMEM),
            pl.BlockSpec(memory_space=pltpu.VMEM),
        ],
        out_specs=(pl.BlockSpec(memory_space=pltpu.VMEM),) * 2,
        scratch_shapes=[pltpu.VMEM((plan.count, BLK, tok), f32)],
        compiler_params=pltpu.CompilerParams(vmem_limit_bytes=VMEM_BYTES),
        name="attn_forward",
    )(rand, rank, kv)


def attn_backward_kernel(
    plan, rand_ref, rank_ref, kv_ref, dout_ref, lse_ref, out_ref, sum_ref, prob_ref, dprob_ref
):
    tok = plan.blocks * BLK
    rank = rank_ref[0]
    out_ref[:, 0:128] = jnp.zeros((plan.count * tok, 128), bf16)
    sum_ref[...] = jnp.zeros_like(sum_ref)

    def operands(half, owner, inner, unit):
        rows = pl.multiple_of(owner * plan.stride + inner * BLK, 16)
        q = only_half(kv_ref[pl.ds(rows, BLK), 0:128], half) * 0.125
        drows = pl.multiple_of(owner * tok + inner * BLK, BLK)
        dout = only_half(dout_ref[pl.ds(drows, BLK), :], half)
        lse = lse_ref[pl.ds(pl.multiple_of(unit * BLK, BLK), BLK), :][:, 0:1]
        return q, dout, lse

    def emit(half, owner, inner, grad_query):
        out_ref[
            pl.ds(pl.multiple_of(owner * tok + inner * BLK, BLK), BLK), pl.ds(half * HD, HD)
        ] = (grad_query[:, half * HD : (half + 1) * HD] * 0.125).astype(bf16)

    for half in range(2):
        step = plan.steps[half]
        offset = lax.rem(rank, step) if step > 1 else 0

        def turn_body(turn, carry, half=half, step=step, offset=offset):
            owner = turn * step + offset
            found = []
            for inner in range(plan.blocks):
                ids = plan.named(half, owner, inner, rand_ref)
                rows = [plan.key_rows(i) for i in ids]
                keys = jnp.concatenate([kv_ref[pl.ds(r, BLK), 128:256] for r in rows], axis=0)
                values = jnp.concatenate([kv_ref[pl.ds(r, BLK), 256:384] for r in rows], axis=0)
                q, dout, lse = operands(half, owner, inner, plan.unit(half, turn, inner))
                if inner in (0, plan.blocks - 1):
                    block = owner * plan.blocks + inner
                    edge = (block == 0) | (block == plan.total - 1)
                    dout = dout * jnp.where(edge, 0.0, 1.0).astype(bf16)
                    kept = jnp.where(edge, 0.0, 1.0)
                else:
                    kept = None
                probs = jnp.exp(contract_cols(q, keys) - lse)
                grad_probs = contract_cols(dout, values)
                delta = jnp.sum(probs * grad_probs, axis=-1, keepdims=True)
                grad_scores = (probs * (grad_probs - delta)).astype(bf16)
                emit(half, owner, inner, plain(grad_scores, keys))
                grad_keys = contract_rows(grad_scores, q)
                grad_values = contract_rows(probs.astype(bf16), dout)
                found.append((ids, grad_keys, grad_values))
            for ids, grad_keys, grad_values in found:
                for t, i in enumerate(ids):
                    at = pl.ds(plan.sum_rows(i), BLK)
                    sum_ref[at, 0:128] += grad_keys[t * BLK : (t + 1) * BLK]
                    sum_ref[at, 128:256] += grad_values[t * BLK : (t + 1) * BLK]
            return carry

        lax.fori_loop(0, plan.owners[half], turn_body, 0)

    for half in range(2):
        step = plan.steps[half]
        for owner, inner in ((0, 0), (plan.count - 1, plan.blocks - 1)):

            def whole(half=half, step=step, owner=owner, inner=inner):
                unit = plan.unit(half, owner // step, inner)
                q, dout, lse = operands(half, owner, inner, unit)

                def first_body(o, delta):
                    rows = pl.ds(pl.multiple_of(o * plan.stride, 16), tok)
                    probs = jnp.exp(contract_cols(q, kv_ref[rows, 128:256]) - lse)
                    grad_probs = contract_cols(dout, kv_ref[rows, 256:384])
                    prob_ref[o] = probs
                    dprob_ref[o] = grad_probs
                    return delta + jnp.sum(probs * grad_probs, axis=-1, keepdims=True)

                delta = lax.fori_loop(0, plan.count, first_body, jnp.zeros((BLK, 1), f32))

                def second_body(o, grad_query):
                    rows = pl.ds(pl.multiple_of(o * plan.stride, 16), tok)
                    at = pl.ds(pl.multiple_of(o * tok, tok), tok)
                    probs = prob_ref[o]
                    grad_scores = (probs * (dprob_ref[o] - delta)).astype(bf16)
                    sum_ref[at, 0:128] += contract_rows(grad_scores, q)
                    sum_ref[at, 128:256] += contract_rows(probs.astype(bf16), dout)
                    return grad_query + plain(grad_scores, kv_ref[rows, 128:256])

                emit(
                    half,
                    owner,
                    inner,
                    lax.fori_loop(0, plan.count, second_body, jnp.zeros((BLK, 128), f32)),
                )

            if step == 1:
                whole()
            else:
                pl.when(lax.rem(rank, step) == owner % step)(whole)

    out_ref[:, 128:384] = sum_ref[...].astype(bf16)


def attn_backward(plan, rand, rank, kv, dout, lse):
    tok = plan.blocks * BLK
    return pl.pallas_call(
        functools.partial(attn_backward_kernel, plan),
        out_shape=jax.ShapeDtypeStruct((plan.count * tok, 384), bf16),
        in_specs=[
            pl.BlockSpec(memory_space=pltpu.SMEM),
            pl.BlockSpec(memory_space=pltpu.SMEM),
            pl.BlockSpec(memory_space=pltpu.VMEM),
            pl.BlockSpec(memory_space=pltpu.VMEM),
            pl.BlockSpec(memory_space=pltpu.VMEM),
        ],
        out_specs=pl.BlockSpec(memory_space=pltpu.VMEM),
        scratch_shapes=[
            pltpu.VMEM((plan.count * tok, 256), f32),
            pltpu.VMEM((plan.count, BLK, tok), f32),
            pltpu.VMEM((plan.count, BLK, tok), f32),
        ],
        compiler_params=pltpu.CompilerParams(vmem_limit_bytes=VMEM_BYTES),
        name="attn_backward",
    )(rand, rank, kv, dout, lse)


def swap(value, axis):
    return lax.all_to_all(value, axis, split_axis=0, concat_axis=0, tiled=True)


def gather_small(shard):
    ny, nc, nz, nx = (lax.axis_size(a) for a in ALL)
    rows, cols = shard.shape
    line = swap(jnp.broadcast_to(shard[None], (nz, rows, cols)), "z")
    plane = swap(jnp.broadcast_to(line[None], (ny * nx, nz, rows, cols)), ("y", "x"))
    both = swap(jnp.broadcast_to(plane[None], (nc, ny * nx, nz, rows, cols)), "core")
    return (
        both.reshape(nc, ny, nx, nz, rows, cols)
        .transpose(1, 0, 3, 2, 4, 5)
        .reshape(ny * nc * nz * nx * rows, cols)
    )


def scatter_small(value):
    ny, nc, nz, nx = (lax.axis_size(a) for a in ALL)
    cols = value.shape[1]
    rows = value.shape[0] // (ny * nc * nz * nx)
    parts = value.reshape(ny, nc, nz, nx, rows, cols).transpose(1, 0, 3, 2, 4, 5)
    parts = parts.astype(bf16).reshape(nc, ny * nx, nz, rows, cols)
    parts = jnp.sum(swap(parts, "core").astype(f32), axis=0).astype(bf16)
    parts = jnp.sum(swap(parts, ("y", "x")).astype(f32), axis=0).astype(bf16)
    return jnp.sum(swap(parts, "z").astype(f32), axis=0)


def body(
    tokens,
    qkv_weight,
    query_bias,
    value_bias,
    out_weight,
    out_bias,
    attn_gain,
    attn_shift,
    up_weight,
    up_bias,
    down_weight,
    down_bias,
    ffn_gain,
    ffn_shift,
    random_blocks,
    cotangent,
):
    count = lax.axis_size("z") * lax.axis_size("x")
    ranks = count // GROUPS
    _, tok, width = tokens.shape
    blocks = tok // BLK
    plan = Plan(count, ranks, blocks)
    ctx_index = lax.axis_index("z") * lax.axis_size("x") + lax.axis_index("x")
    rank = lax.rem(ctx_index, ranks).astype(jnp.int32).reshape(1)
    rows = qkv_weight.shape[0]
    hidden = up_weight.shape[1]
    flat_tokens = tokens.reshape(tok, width)

    small = [query_bias, value_bias, out_bias, attn_gain, attn_shift, down_bias, ffn_gain, ffn_shift]
    columns = jnp.concatenate(
        [jnp.stack(small, axis=1), up_bias.reshape(rows, hidden // width)], axis=1
    )
    columns = jnp.pad(columns, ((0, 0), (0, EXTRA - columns.shape[1])))
    qkv_ext = gather_small(jnp.concatenate([qkv_weight, columns], axis=1))
    qkv_full = qkv_ext[:, : 3 * width]
    biases = qkv_ext[:, 3 * width :].astype(f32)
    vectors = biases[:, :8].T
    up_bias_full = biases[:, 8 : 8 + hidden // width].reshape(1, hidden)
    packed = jnp.concatenate(
        [out_weight, up_weight, down_weight.reshape(rows, -1)], axis=1
    )
    packed_full = lax.all_gather(packed, ALL, axis=0, tiled=True)
    out_full = packed_full[:, :width]
    up_full = packed_full[:, width : width + hidden]
    down_full = packed_full[:, width + hidden :].reshape(hidden, width)

    picks = random_blocks[0].astype(bf16)
    rnd = []
    for j in range(count):
        first, shared = heads_of(j, ranks)
        rnd.append(jnp.stack([picks[:, first], picks[:, shared]], axis=1).reshape(-1))
    rnd = jnp.stack(rnd)
    entries = rnd.shape[1]
    rnd = jnp.pad(rnd[:, None, :], ((0, 0), (0, PAD_ROWS - 1), (0, 384 - entries)))

    qkv_bias = jnp.stack([vectors[0], jnp.zeros_like(vectors[0]), vectors[1]])
    chunks = qkv_chunks(count, ranks, flat_tokens, qkv_full, qkv_bias, rnd)
    kv = swap(chunks, CTX)
    rand = kv[:, tok, :entries].astype(jnp.int32).reshape(-1)
    kv = kv.reshape(count * plan.stride, 384)
    attended, lse = attn_forward(plan, rand, rank, kv)
    back = swap(attended.reshape(count, tok, 128), CTX)
    back = back.reshape(GROUPS, ranks, tok, 2, HD)
    half_ranks = ranks // 2

    def add(values):
        return values[:, 0] if values.shape[1] == 1 else jnp.sum(values, axis=1)

    attn_low = (
        jnp.stack(
            [
                add(back[:, :half_ranks, :, 0]),
                add(back[:, half_ranks:, :, 0]),
                add(back[:, :, :, 1]),
            ],
            axis=1,
        )
        .transpose(2, 0, 1, 3)
        .reshape(tok, width)
    )

    branch = plain(attn_low, out_full) + vectors[2]
    mid_norm, mid_pull = jax.vjp(
        layer_norm, flat_tokens.astype(f32) + branch, vectors[3], vectors[4]
    )
    mid_low = mid_norm.astype(bf16)
    pre_act = plain(mid_low, up_full) + up_bias_full
    activation, gelu_pull = jax.vjp(gelu_tanh, pre_act)
    act_low = activation.astype(bf16)
    branch_two = plain(act_low, down_full) + vectors[5]
    final_norm, final_pull = jax.vjp(layer_norm, mid_norm + branch_two, vectors[6], vectors[7])
    output = final_norm.astype(bf16).reshape(1, tok, width)
    grad_final, grad_ffn_gain, grad_ffn_shift = final_pull(
        cotangent.reshape(tok, width).astype(f32)
    )
    down_low = grad_final.astype(bf16)
    grad_down_bias = jnp.sum(down_low.astype(f32), axis=0)
    grad_down = contract_rows(act_low, down_low).astype(bf16)
    (grad_pre,) = gelu_pull(contract_cols(down_low, down_full))
    pre_low = grad_pre.astype(bf16)
    grad_up_bias = jnp.sum(pre_low.astype(f32), axis=0)
    grad_up = contract_rows(mid_low, pre_low).astype(bf16)
    grad_mid = grad_final + contract_cols(pre_low, up_full)
    grad_resid, grad_attn_gain, grad_attn_shift = mid_pull(grad_mid)
    branch_low = grad_resid.astype(bf16)
    grad_out_bias = jnp.sum(branch_low.astype(f32), axis=0)
    grad_out = contract_rows(attn_low, branch_low).astype(bf16)
    grad_attn = contract_cols(branch_low, out_full).astype(bf16)

    tiles = grad_attn.reshape(tok, H, HD)
    dout = []
    for j in range(count):
        first, shared = heads_of(j, ranks)
        dout.append(jnp.concatenate([tiles[:, first], tiles[:, shared]], axis=1))
    dout = swap(jnp.stack(dout), CTX).reshape(count * tok, 128)
    grads = attn_backward(plan, rand, rank, kv, dout, lse)
    grads = swap(grads.reshape(count, tok, 384), CTX)
    grads = grads.reshape(GROUPS, ranks, tok, 3, 2, HD).astype(f32)
    qkv_grad_low = (
        jnp.stack(
            [
                add(grads[:, :half_ranks, :, :, 0]),
                add(grads[:, half_ranks:, :, :, 0]),
                add(grads[:, :, :, :, 1]),
            ],
            axis=1,
        )
        .astype(bf16)
        .transpose(2, 3, 0, 1, 4)
        .reshape(tok, 3 * width)
    )
    column_sums = jnp.sum(qkv_grad_low.astype(f32), axis=0)
    grad_qkv = contract_rows(flat_tokens, qkv_grad_low).astype(bf16)
    tokens_grad = (grad_resid + contract_cols(qkv_grad_low, qkv_full)).reshape(1, tok, width)

    wide = lax.psum_scatter(
        jnp.concatenate([grad_out, grad_up, grad_down.reshape(width, -1)], axis=1),
        ALL,
        scatter_dimension=0,
        tiled=True,
    ).astype(f32)
    grad_small = jnp.stack(
        [
            column_sums[:width],
            column_sums[2 * width :],
            grad_out_bias,
            grad_attn_gain,
            grad_attn_shift,
            grad_down_bias,
            grad_ffn_gain,
            grad_ffn_shift,
        ],
        axis=1,
    )
    grad_columns = jnp.concatenate(
        [grad_small, grad_up_bias.reshape(width, hidden // width)], axis=1
    ).astype(bf16)
    grad_columns = jnp.pad(grad_columns, ((0, 0), (0, EXTRA - grad_columns.shape[1])))
    tail = scatter_small(jnp.concatenate([grad_qkv, grad_columns], axis=1))
    shards = tail[:, 3 * width :]
    return (
        output,
        tokens_grad,
        tail[:, : 3 * width],
        shards[:, 0],
        shards[:, 1],
        wide[:, :width],
        shards[:, 2],
        shards[:, 3],
        shards[:, 4],
        wide[:, width : width + hidden],
        shards[:, 8 : 8 + hidden // width].reshape(-1),
        wide[:, width + hidden :].reshape(-1, width),
        shards[:, 5],
        shards[:, 6],
        shards[:, 7],
    )


def solution(mesh):
    dp, ctx = (mesh.shape[a] for a in ("dp", "ctx"))
    fine = Mesh(mesh.devices.reshape(dp // 2, 2, ctx // 2, 2), ALL)
    seqs, ranges, shards = ("y", "core"), CTX, ALL
    token_spec = P(seqs, ranges, None)
    return jax.shard_map(
        body,
        mesh=fine,
        in_specs=(
            token_spec,
            P(shards, None),
            P(shards),
            P(shards),
            P(shards, None),
            P(shards),
            P(shards),
            P(shards),
            P(shards, None),
            P(shards),
            P(shards, None),
            P(shards),
            P(shards),
            P(shards),
            P(seqs, ranges, None, None),
            token_spec,
        ),
        out_specs=(
            token_spec,
            token_spec,
            P(shards, None),
            P(shards),
            P(shards),
            P(shards, None),
            P(shards),
            P(shards),
            P(shards),
            P(shards, None),
            P(shards),
            P(shards, None),
            P(shards),
            P(shards),
            P(shards),
        ),
        check_vma=False,
    )
```

time: 1290 us -> 468 us (0.36)
  waiting for transfers between devices: 752 us -> 150 us
  Pallas kernels: 0 us -> 73.3 us
  local copies, waits for them, and re-layouts: 135 us -> 62.5 us
  matrix products: 105 us -> 33 us
  blocking collectives: 160 us -> 89.2 us
  other arithmetic: 89.5 us -> 23.7 us
    reduce_scatter x3 -> x1, waiting for transfers between devices: 245 us -> 0.01 us  [body(): lax.psum_scatter(jnp.concatenate([grad_out, grad_up, grad_down.reshape(wi...]
    all_gather x4 -> x1, waiting for transfers between devices: 172 us -> 0.02 us  [body(): packed_full = lax.all_gather(packed, ALL, axis=0, tiled=True)]
    unnamed x13 -> x2, waiting for transfers between devices: 128 us -> 0.03 us
    psum x4 -> x0, waiting for transfers between devices: 115 us -> none  [the longest x1 65.4 us: body(): global_dout = lax.psum(dout_term.astype(jnp.bfloat16), 'ctx')]
    unnamed x2 -> x0, blocking collectives: 89.1 us -> none
    all_to_all x1 -> x5, blocking collectives: 10.1 us -> 89.2 us  [swap(): return lax.all_to_all(value, axis, split_axis=0, concat_axis=0, tiled=True)]
    all_to_all x2 -> x5, waiting for transfers between devices: 72.2 us -> 150 us  [swap(): return lax.all_to_all(value, axis, split_axis=0, concat_axis=0, tiled=True)]
    pallas_call x0 -> x3, Pallas kernels: none -> 73.3 us  [the longest x1 36.7 us: attn_backward(): pl.pallas_call(functools.partial(attn_backward_kernel, plan), out_shape=j...]
  transfers between devices with their start and end apart: 18 -> 7, of which waited for: 14 -> 5; matrix products, arithmetic and copies ran while one was open for 18% -> 11% of each run, Pallas kernels for 0% -> 16%
where the time goes in v1:
time: 468 us; the launch traced here: 466 us
  waiting for transfers between devices  150 us (32%)
  blocking collectives  89.2 us (19%)
  Pallas kernels  73.3 us (16%)
  local copies, waits for them, and re-layouts  62.5 us (13%)
  matrix products  33 us (7%)
  other arithmetic  23.7 us (5%)
  starting transfers between devices  20.5 us (4%)
  between operations  14.6 us (3%)
    all_to_all x5, waiting for transfers between devices, swap(): return lax.all_to_all(value, axis, split_axis=0, concat_axis=0, tiled=True)  150 us
    all_to_all x5, blocking collectives, swap(): return lax.all_to_all(value, axis, split_axis=0, concat_axis=0, tiled=True)  89.2 us
    pallas_call x1, Pallas kernels, attn_backward(): pl.pallas_call(functools.partial(attn_backward_kernel, plan), out_shape=j...  36.7 us
    pallas_call x1, Pallas kernels, attn_forward(): pl.pallas_call(functools.partial(attn_forward_kernel, plan), out_shape=(j...  32.1 us
    all_to_all x5, starting transfers between devices, swap(): return lax.all_to_all(value, axis, split_axis=0, concat_axis=0, tiled=True)  20.3 us
    dot_general x4, matrix products, contract_cols(): lax.dot_general(left_side, right_side, (((1,), (1,)), ((), ())), preferre...  15.2 us
    dot_general x4, matrix products, contract_rows(): lax.dot_general(left_side, right_side, (((0,), (0,)), ((), ())), preferre...  9.92 us
  transfers between devices with their start and end apart: 7, of which 5 were waited for; matrix products, arithmetic and copies ran while one was open for 11% of the time, Pallas kernels for 16%

profile of v1, /device:TPU:0, one launch (start us, length us, event | category | flops | bytes accessed | tf_op | source)
XLA Modules:
  0.0 466.4 jit_solution(6075890487340704157)
XLA Ops:
  17.7 26.2 %all_to_all.50 = bf16[4,24,2432]{2,1,0:T(8,128)(2,1)S(1)} all-to-all(bf16[4,24,2432]{2,1,0:T(8,128)(2,1)S(1)} %broadcast_in_dim.16), channel_id=1, replica_groups=mesh['y'=2,'core'=2,'z'=4,'x'=2] {'z'}, dimensions={0} | all-to-all | bytes 933888 | tf_op jit(solution)/shard_map/all_to_all | solution.py:360
  51.8 26.7 %all-to-all-done.1 = bf16[4,4,24,2432]{3,2,1,0:T(8,128)(2,1)S(1)} async-done(((bf16[4,4,24,2432]{3,2,1,0:T(8,128)(2,1)}), bf16[4,4,24,2432]{3,2,1,0:T(8,128)(2,1)S(1)}, u32[]{:S(2)}, u32[]{:S(2)}) %all-to-all-start.1) | async-done | bytes 1867808 | tf_op jit(solution)/shard_map/all_to_all | solution.py:360
  78.8 7.5 %all_to_all.51 = bf16[2,4,4,24,2432]{4,3,2,1,0:T(8,128)(2,1)S(1)} all-to-all(bf16[2,4,4,24,2432]{4,3,2,1,0:T(8,128)(2,1)S(1)} %broadcast_in_dim.18), channel_id=1, replica_groups=mesh['y'=2,'core'=2,'z'=4,'x'=2] {'core'}, dimensions={0} | all-to-all | bytes 7471104 | tf_op jit(solution)/shard_map/all_to_all | solution.py:360
  91.5 4.5 qkv_chunks.1
  96.0 5.8 %all-to-all-start.3 = ((bf16[8,272,384]{2,1,0:T(8,128)(2,1)}), bf16[8,272,384]{2,1,0:T(8,128)(2,1)S(1)}, u32[]{:S(2)}, u32[]{:S(2)}) async-start(bf16[8,272,384]{2,1,0:T(8,128)(2,1)} %qkv_chunks.1), calls=%async_computation.3 | async-start | bytes 3342336 | tf_op jit(solution)/shard_map/all_to_all | solution.py:360
  101.7 48.5 %all-to-all-done.3 = bf16[8,272,384]{2,1,0:T(8,128)(2,1)S(1)} async-done(((bf16[8,272,384]{2,1,0:T(8,128)(2,1)}), bf16[8,272,384]{2,1,0:T(8,128)(2,1)S(1)}, u32[]{:S(2)}, u32[]{:S(2)}) %all-to-all-start.3) | async-done | bytes 1671200 | tf_op jit(solution)/shard_map/all_to_all | solution.py:360
  151.4 32.1 %attn_forward.1 = (bf16[2048,128]{1,0:T(8,128)(2,1)}, f32[3072,128]{1,0:T(8,128)}) custom-call(s32[192]{0:T(256)} %reshape.207.rand_ref, s32[1]{0:T(128)} %bitcast.15.rank_ref, bf16[2176,384]{1,0:T(8,128)(2,1)} %bitcast.135), custom_call_target="tpu_custom_call" | custom-call | tf_op jit(solution)/shard_map/attn_forward/pallas_call | solution.py:218
  189.7 14.2 %all-to-all-done.4 = bf16[8,256,128]{1,2,0:T(8,128)(2,1)S(1)} async-done(((bf16[8,256,128]{1,2,0:T(8,128)(2,1)}), bf16[8,256,128]{1,2,0:T(8,128)(2,1)S(1)}, u32[]{:S(2)}, u32[]{:S(2)}) %all-to-all-start.4) | async-done | bytes 524320 | tf_op jit(solution)/shard_map/all_to_all | solution.py:360
  204.1 4.9 %slice.287 = bf16[768,3072]{1,0:T(8,128)(2,1)} slice(bf16[768,6912]{1,0:T(8,128)(2,1)} %all-gather.2.cloned.1.call-done), slice={[0:768], [3840:6912]} | slice | bytes 9437184 | tf_op jit(solution)/shard_map/slice | solution.py:432
  209.0 8.5 %reshape.194 = bf16[3072,768]{1,0:T(8,128)(2,1)} reshape(bf16[768,3072]{1,0:T(8,128)(2,1)} %slice.287) | data formatting | bytes 9437184 | tf_op jit(solution)/shard_map/reshape | solution.py:432
  227.7 4.5 fusion.55
  232.2 4.5 convolution_convert_fusion
  240.6 4.7 multiply_reduce_fusion
  245.6 8.8 %reshape.204 = bf16[768,3072]{1,0:T(8,128)(2,1)} reshape(bf16[3072,768]{1,0:T(8,128)(2,1)} %convolution_convert_fusion) | data formatting | bytes 9437184 | tf_op jit(solution)/shard_map/reshape | solution.py:524
  255.7 8.8 %pad_maximum_fusion = bf16[768,6912]{1,0:T(8,128)(2,1)} fusion(bf16[768,3072]{1,0:T(8,128)(2,1)} %reshape.204, bf16[768,3072]{1,0:T(8,128)(2,1)} %convolution_convert_fusion.1, bf16[768,768]{1,0:T(8,128)(2,1)S(1)} %copy.162), kind=kLoop, calls=%fused_computation | loop fusion | flops 31850496 | bytes 21233664 | tf_op jit(solution)/shard_map/concatenate | solution.py:524
  266.6 18.1 %all_to_all.52 = bf16[8,256,128]{1,2,0:T(8,128)(2,1)S(1)} all-to-all(bf16[8,256,128]{1,2,0:T(8,128)(2,1)S(1)} %fusion.35), channel_id=1, replica_groups=mesh['y'=2,'core'=2,'z'=4,'x'=2] {'z','x'}, dimensions={0} | all-to-all | bytes 1048576 | tf_op jit(solution)/shard_map/all_to_all | solution.py:360
  285.7 36.7 %attn_backward.1 = bf16[2048,384]{1,0:T(8,128)(2,1)} custom-call(s32[192]{0:T(256)} %reshape.207.rand_ref, s32[1]{0:T(128)} %bitcast.15.rank_ref, bf16[2176,384]{1,0:T(8,128)(2,1)} %bitcast.136, bf16[2048,128]{1,0:T(8,128)(2,1)} %bitcast.150, f32[3072,128]{1,0:T(8,128)} %get-tuple-element.18.lse_ref), custom_call_target="tpu_custom_call" | custom-call | tf_op jit(solution)/shard_map/attn_backward/pallas_call | solution.py:338
  329.6 51.9 %all-to-all-done.6 = bf16[8,256,384]{1,2,0:T(8,128)(2,1)S(1)} async-done(((bf16[8,256,384]{1,2,0:T(8,128)(2,1)}), bf16[8,256,384]{1,2,0:T(8,128)(2,1)S(1)}, u32[]{:S(2)}, u32[]{:S(2)}) %all-to-all-start.6) | async-done | bytes 1572896 | tf_op jit(solution)/shard_map/all_to_all | solution.py:360
  385.8 6.1 %copy.160 = bf16[768,2432]{1,0:T(8,128)(2,1)} copy(bf16[768,2432]{0,1:T(8,128)(2,1)} %fusion.9) | data formatting | bytes 7471104 | tf_op jit(solution)/shard_map/concatenate | solution.py:546
  394.2 7.7 %all_to_all.53 = bf16[2,4,4,24,2432]{4,3,2,1,0:T(8,128)(2,1)} all-to-all(bf16[2,4,4,24,2432]{4,3,2,1,0:T(8,128)(2,1)S(1)} %bitcast.142), channel_id=1, replica_groups=mesh['y'=2,'core'=2,'z'=4,'x'=2] {'core'}, dimensions={0} | all-to-all | bytes 7471104 | tf_op jit(solution)/shard_map/all_to_all | solution.py:360
  401.9 4.6 reduce_sum.248
  406.6 29.7 %all_to_all.54 = bf16[4,4,24,2432]{3,2,1,0:T(8,128)(2,1)S(1)} all-to-all(bf16[4,4,24,2432]{3,2,1,0:T(8,128)(2,1)} %reduce_sum.248), channel_id=1, replica_groups=mesh['y'=2,'core'=2,'z'=4,'x'=2] {'y','x'}, dimensions={0} | all-to-all | bytes 3735552 | tf_op jit(solution)/shard_map/all_to_all | solution.py:360
  440.9 4.2 fusion.20
  445.1 8.3 %all-to-all-done.9 = bf16[4,24,2432]{2,1,0:T(8,128)(2,1)S(1)} async-done(((bf16[4,24,2432]{2,1,0:T(8,128)(2,1)}), bf16[4,24,2432]{2,1,0:T(8,128)(2,1)S(1)}, u32[]{:S(2)}, u32[]{:S(2)}) %all-to-all-start.9) | async-done | bytes 466976 | tf_op jit(solution)/shard_map/all_to_all | solution.py:360
  (157 shorter events, 74.4 us)
Async XLA Ops:
  7.2 197.0 %all-gather.2.cloned.1.call-start = ((), (), s32[]{:S(2)}) async-start(), calls=%async_computation.11 | async-start | bytes 10948608 | tf_op jit(solution)/shard_map/all_gather | solution.py:429
  44.0 5.0 %copy-start.6 = (s32[1,4,12,3]{2,1,3,0:T(4,128)S(1)}, s32[1,4,12,3]{2,1,3,0:T(4,128)}, u32[]{:S(2)}) copy-start(s32[1,4,12,3]{2,1,3,0:T(4,128)} %param.30) | copy-start | bytes 1732
  45.3 33.3 %all-to-all-start.1 = ((bf16[4,4,24,2432]{3,2,1,0:T(8,128)(2,1)}), bf16[4,4,24,2432]{3,2,1,0:T(8,128)(2,1)S(1)}, u32[]{:S(2)}, u32[]{:S(2)}) async-start(bf16[4,4,24,2432]{3,2,1,0:T(8,128)(2,1)} %broadcast_in_dim.17), calls=%async_computation.1 | async-start | bytes 3735552 | tf_op jit(solution)/shard_map/all_to_all | solution.py:360
  86.6 1.8 copy-start.1
  96.0 54.2 %all-to-all-start.3 = ((bf16[8,272,384]{2,1,0:T(8,128)(2,1)}), bf16[8,272,384]{2,1,0:T(8,128)(2,1)S(1)}, u32[]{:S(2)}, u32[]{:S(2)}) async-start(bf16[8,272,384]{2,1,0:T(8,128)(2,1)} %qkv_chunks.1), calls=%async_computation.3 | async-start | bytes 3342336 | tf_op jit(solution)/shard_map/all_to_all | solution.py:360
  150.2 1.2 copy-start
  185.6 18.4 %all-to-all-start.4 = ((bf16[8,256,128]{1,2,0:T(8,128)(2,1)}), bf16[8,256,128]{1,2,0:T(8,128)(2,1)S(1)}, u32[]{:S(2)}, u32[]{:S(2)}) async-start(bf16[8,256,128]{1,2,0:T(8,128)(2,1)} %copy.148), calls=%async_computation.4 | async-start | bytes 1048576 | tf_op jit(solution)/shard_map/all_to_all | solution.py:360
  189.1 266.6 %reduce-scatter.2.cloned.1.call-start = ((), (), s32[]{:S(2)}) async-start(), calls=%async_computation.12 | async-start | bytes 10948608 | tf_op jit(solution)/shard_map/reduce_scatter | solution.py:523
  209.0 8.5 %copy-start.4 = (bf16[1,256,768]{2,1,0:T(8,128)(2,1)S(1)}, bf16[1,256,768]{2,1,0:T(8,128)(2,1)}, u32[]{:S(2)}) copy-start(bf16[1,256,768]{2,1,0:T(8,128)(2,1)} %param.16) | copy-start | bytes 1179652
  219.4 4.2 slice-start
  219.7 4.0 slice-start.1
  223.7 2.3 copy-start.2
  245.6 8.8 %copy-start.3 = (f32[256,768]{1,0:T(8,128)}, f32[256,768]{1,0:T(8,128)S(1)}, u32[]{:S(2)}) copy-start(f32[256,768]{1,0:T(8,128)S(1)} %get-tuple-element.47) | copy-start | bytes 2359300
  322.4 6.6 %copy-start.8 = (bf16[768]{0:T(1024)(128)(2,1)S(1)}, bf16[768]{0:T(1024)(128)(2,1)}, u32[]{:S(2)}) copy-start(bf16[768]{0:T(1024)(128)(2,1)} %get-tuple-element.19) | copy-start | bytes 4612
  322.4 6.6 %copy-start.7 = (bf16[768]{0:T(1024)(128)(2,1)S(1)}, bf16[768]{0:T(1024)(128)(2,1)}, u32[]{:S(2)}) copy-start(bf16[768]{0:T(1024)(128)(2,1)} %get-tuple-element.23) | copy-start | bytes 4612
  322.4 6.7 %copy-start.5 = (bf16[3072]{0:T(1024)(128)(2,1)S(1)}, bf16[3072]{0:T(1024)(128)(2,1)}, u32[]{:S(2)}) copy-start(bf16[3072]{0:T(1024)(128)(2,1)} %get-tuple-element.38) | copy-start | bytes 18436
  325.0 56.5 %all-to-all-start.6 = ((bf16[8,256,384]{1,2,0:T(8,128)(2,1)}), bf16[8,256,384]{1,2,0:T(8,128)(2,1)S(1)}, u32[]{:S(2)}, u32[]{:S(2)}) async-start(bf16[8,256,384]{1,2,0:T(8,128)(2,1)} %copy.154), calls=%async_computation.6 | async-start | bytes 3145728 | tf_op jit(solution)/shard_map/all_to_all | solution.py:360
  437.4 16.0 %all-to-all-start.9 = ((bf16[4,24,2432]{2,1,0:T(8,128)(2,1)}), bf16[4,24,2432]{2,1,0:T(8,128)(2,1)S(1)}, u32[]{:S(2)}, u32[]{:S(2)}) async-start(bf16[4,24,2432]{2,1,0:T(8,128)(2,1)} %reduce_sum.249), calls=%async_computation.9 | async-start | bytes 933888 | tf_op jit(solution)/shard_map/all_to_all | solution.py:360
Sparse Core Ops, SparseCore 0:
  11.6 113.4 all-gather.1
  264.6 166.3 reduce-scatter.1
